TPU v7x, 256 devices: a whole 4x4x8 slice. The times are simulated.
256 devices in a mesh: coil: 32 (over z, y), slab: 8 (over x, core).
Axes of the slice: x: 4, y: 4, z: 8, core: 2. Of those that a mesh axis runs over, the one named last changes fastest.
Arguments:
- cotangent: float32 [32, 2, 256, 256], P('coil', None, 'slab'), may hold values from -60 to 60
- saved_solution: float32 [32, 2, 256, 256], P('coil', None, 'slab'), may hold values from -6 to 6
- coil_maps: bfloat16 [32, 32, 2, 256, 256], P('coil', None, None, 'slab'), may hold values from -1.5 to 1.5
- kspace: bfloat16 [32, 32, 2, 256, 256], P('coil', None, None, 'slab'), may hold values from -6 to 6
- mask_logit: float32 [32, 256], P(None, 'slab'), may hold values from -4.5 to 4.5
- reach: int32 [32, 256], P(None, 'slab'), may hold values from 0 to 256, as said below
Outputs:
- image_grad: float32 [32, 2, 256, 256], P('coil', None, 'slab')
- kspace_grad: bfloat16 [32, 32, 2, 256, 256], P('coil', None, None, 'slab')
- logit_grad: float32 [32, 256], P(None, 'slab')
Inputs may be any that keep to these rules, and one draw needn't show every extreme that they name: reach[z, y] is 0 (line not acquired) or between 128 and 256; line [0, 0] is always fully acquired and line [0, 128] never.
All inputs are finite; a program needn't handle non-finite values.
Results may differ from a plain program's by a relative error of at most 0.02.
Values may be sent and summed in bfloat16 or wider, within the bound.
A program may use at most 64 MiB of HBM per device.

v0:
```python
import math
import jax
import jax.numpy as jnp
from jax import lax
from jax.sharding import PartitionSpec as P

NX = 256
NY = 256
NZ = 32
ITERS = 2
DAMPING = 0.2


def dft_table(length, sign):
    index = jnp.arange(length, dtype=jnp.int32)
    phase = (index[:, None] * index[None, :] % length).astype(jnp.float32) * (
        2.0 * math.pi / length
    )
    factor = 1.0 / math.sqrt(length)
    cosine = jnp.cos(phase) * factor
    sine = sign * jnp.sin(phase) * factor
    table = jnp.stack(
        [jnp.stack([cosine, sine], axis=1), jnp.stack([-sine, cosine], axis=1)], axis=0
    )
    return table.astype(jnp.bfloat16)


def complex_product(factor, operand):
    factor_re, factor_im = (factor[:, 0], factor[:, 1])
    operand_re, operand_im = (operand[:, 0], operand[:, 1])
    return jnp.stack(
        [
            factor_re * operand_re - factor_im * operand_im,
            factor_re * operand_im + factor_im * operand_re,
        ],
        axis=1,
    )


def conjugate_product(factor, operand):
    factor_re, factor_im = (factor[:, 0], factor[:, 1])
    operand_re, operand_im = (operand[:, 0], operand[:, 1])
    return jnp.stack(
        [
            factor_re * operand_re + factor_im * operand_im,
            factor_re * operand_im - factor_im * operand_re,
        ],
        axis=1,
    )


def shards(cotangent, saved_solution, coil_maps, kspace, mask_logit, reach):
    y_fwd, y_inv = (dft_table(NY, -1.0), dft_table(NY, 1.0))
    z_fwd, z_inv = (dft_table(NZ, -1.0), dft_table(NZ, 1.0))
    x_fwd, x_inv = (dft_table(NX, -1.0), dft_table(NX, 1.0))
    maps = coil_maps[0]
    data = kspace[0].astype(jnp.float32)
    readout = jnp.arange(NX, dtype=jnp.int32)
    centred = (readout + NX // 2) % NX
    sampled = (centred[None, None, :] >= (NX - reach)[:, :, None]).astype(jnp.float32)
    gate = jax.nn.sigmoid(mask_logit)
    weight = sampled * gate[:, :, None]
    squared = (weight * weight)[:, None]

    def front(piece):
        product = complex_product(maps.astype(jnp.float32), piece.astype(jnp.float32)).astype(
            jnp.bfloat16
        )
        return jnp.einsum(
            "zixn,inok->zoxk", product, y_fwd, preferred_element_type=jnp.float32
        ).astype(jnp.bfloat16)

    def gathered_front(shard):
        return front(lax.all_gather(shard, "coil", axis=0, tiled=True))

    def to_kspace(rows):
        mixed = jnp.einsum(
            "nixk,inom->moxk", rows, z_fwd, preferred_element_type=jnp.float32
        ).astype(jnp.bfloat16)
        swapped = lax.all_to_all(mixed, "slab", split_axis=3, concat_axis=2, tiled=True)
        return jnp.einsum("zink,inoq->zokq", swapped, x_fwd, preferred_element_type=jnp.float32)

    direction = cotangent
    both = ("coil", "slab")
    saved_k = to_kspace(gathered_front(saved_solution.astype(jnp.bfloat16)))
    first_k = to_kspace(gathered_front(direction.astype(jnp.bfloat16)))
    first_w = weight[:, None] * first_k
    norm_now, first_energy = lax.psum(
        (jnp.sum(direction * direction), jnp.sum(first_w * first_w)), both
    )
    apply_spectrum = (squared * first_k).astype(jnp.bfloat16)
    to_mixed = jnp.einsum(
        "zikq,iqon->zonk", apply_spectrum, x_inv, preferred_element_type=jnp.float32
    ).astype(jnp.bfloat16)
    to_swapped = lax.all_to_all(to_mixed, "slab", split_axis=2, concat_axis=3, tiled=True)
    apply_image_rows = jnp.einsum(
        "mixk,imon->noxk", to_swapped, z_inv, preferred_element_type=jnp.float32
    ).astype(jnp.bfloat16)
    image = jnp.einsum(
        "zixk,ikon->zoxn", apply_image_rows, y_inv, preferred_element_type=jnp.float32
    )
    summed = lax.psum_scatter(
        conjugate_product(maps.astype(jnp.float32), image).astype(jnp.bfloat16),
        "coil",
        scatter_dimension=0,
        tiled=True,
    ).astype(jnp.float32)
    image = summed + DAMPING * direction
    alpha = norm_now / (first_energy + DAMPING * norm_now)
    residual = direction - alpha * image
    second_k = to_kspace(gathered_front(residual.astype(jnp.bfloat16)))
    second_w = weight[:, None] * second_k
    gain = gate * (1.0 - gate)
    target = data - 2.0 * weight[:, None] * saved_k

    def line_terms(spectrum):
        return gain * jnp.sum(sampled * jnp.sum(spectrum * target, axis=1), axis=2)

    norm_next, crossing, second_energy, mixed_energy = lax.psum(
        (
            jnp.sum(residual * residual),
            jnp.sum(residual * direction),
            jnp.sum(second_w * second_w),
            jnp.sum(second_w * first_w),
        ),
        both,
    )
    lines = lax.psum(jnp.stack([line_terms(first_k), line_terms(second_k)]), "coil")
    beta = norm_next / norm_now
    curvature = (
        second_energy
        + beta * (2.0 * mixed_energy + beta * first_energy)
        + DAMPING * (norm_next + beta * (2.0 * crossing + beta * norm_now))
    )
    later = norm_next / curvature
    early = alpha + later * beta
    image_grad = DAMPING * (early * direction + later * residual)
    kspace_grad = (early * first_w + later * second_w).astype(jnp.bfloat16)[None]
    logit_grad = early * lines[0] + later * lines[1]
    return (image_grad, kspace_grad, logit_grad)


def solution(mesh):
    placed = (
        P("coil", None, "slab", None),
        P("coil", None, "slab", None),
        P("coil", None, None, "slab", None),
        P("coil", None, None, "slab", None),
        P(None, "slab"),
        P(None, "slab"),
    )
    return jax.shard_map(
        shards,
        mesh=mesh,
        in_specs=placed,
        out_specs=(
            P("coil", None, "slab", None),
            P("coil", None, None, "slab", None),
            P(None, "slab"),
        ),
        check_vma=False,
    )
```

profile of v0, /device:TPU:2, one launch (start us, length us, event | category | flops | bytes accessed | tf_op | source)
XLA Modules:
  0.0 753.5 jit_solution(7913596652548034315)
XLA Ops:
  16.2 74.3 %all-gather.4.cloned.1.call-done = bf16[32,2,32,256]{3,2,1,0:T(8,128)(2,1)} async-done(((bf16[1,2,32,256]{3,2,1,0:T(8,128)(2,1)}), bf16[32,2,32,256]{3,2,1,0:T(8,128)(2,1)}) %all-gather.4.cloned.1.call-update) | async-done | bytes 1048592 | tf_op jit(solution)/shard_map/all_gather | solution.py:74
  97.1 7.2 copy.81
  104.3 7.8 %reshape.272 = bf16[8,2,32768]{2,1,0:T(2,128)(2,1)} reshape(bf16[256,2,32,32]{3,2,1,0:T(8,128)(2,1)} %bitcast.296) | data formatting | bytes 2097152
  120.4 11.7 %all-to-all-done = bf16[8,2,32768]{2,1,0:T(2,128)(2,1)} async-done(((bf16[8,2,32768]{2,1,0:T(2,128)(2,1)}), bf16[8,2,32768]{2,1,0:T(2,128)(2,1)}, u32[]{:S(2)}, u32[]{:S(2)}) %all-to-all-start) | async-done | bytes 1048608 | tf_op jit(solution)/shard_map/all_to_all | solution.py:80
  132.1 7.0 reshape.273
  139.1 6.7 copy.82
  158.1 7.2 copy.85
  165.3 7.8 %reshape.274 = bf16[8,2,32768]{2,1,0:T(2,128)(2,1)} reshape(bf16[256,2,32,32]{3,2,1,0:T(8,128)(2,1)} %bitcast.297) | data formatting | bytes 2097152
  182.1 11.2 %all-to-all-done.1 = bf16[8,2,32768]{2,1,0:T(2,128)(2,1)} async-done(((bf16[8,2,32768]{2,1,0:T(2,128)(2,1)}), bf16[8,2,32768]{2,1,0:T(2,128)(2,1)}, u32[]{:S(2)}, u32[]{:S(2)}) %all-to-all-start.1) | async-done | bytes 1048608 | tf_op jit(solution)/shard_map/all_to_all | solution.py:95
  193.3 7.0 reshape.275
  200.4 6.9 copy.160
  221.5 73.8 %all-reduce.2 = (f32[]{:T(128)}, f32[]{:T(128)}) all-reduce(f32[]{:T(128)} %get-tuple-element.49, f32[]{:T(128)} %get-tuple-element.40), channel_id=1, replica_groups=mesh['coil'=32,'slab'=8] {'coil','slab'}, use_global_device_ids=true, to_apply=%region_1.2 | all-reduce | flops 2 | bytes 16 | tf_op jit(solution)/shard_map/psum | solution.py:88
  297.2 71.0 %all-reduce.5.cloned.1.call-done = bf16[32,2,32,256]{3,2,0,1:T(8,128)(2,1)} async-done(((bf16[32,2,32,256]{3,2,0,1:T(8,128)(2,1)}), bf16[32,2,32,256]{3,2,0,1:T(8,128)(2,1)}) %all-reduce.5.cloned.1.call-update) | async-done | bytes 1048592
  374.1 7.2 copy.103
  381.4 7.8 %reshape.278 = bf16[8,2,32768]{2,1,0:T(2,128)(2,1)} reshape(bf16[256,2,32,32]{3,2,1,0:T(8,128)(2,1)} %bitcast.298) | data formatting | bytes 2097152
  394.3 50.5 %all-gather.6.cloned.1.call-done = bf16[32,2,32,256]{3,2,1,0:T(8,128)(2,1)} async-done(((bf16[1,2,32,256]{3,2,1,0:T(8,128)(2,1)}), bf16[32,2,32,256]{3,2,1,0:T(8,128)(2,1)}) %all-gather.6.cloned.1.call-update) | async-done | bytes 1048592 | tf_op jit(solution)/shard_map/all_gather | solution.py:74
  450.5 6.5 copy.97
  457.0 7.8 %reshape.276 = bf16[8,2,32768]{2,1,0:T(2,128)(2,1)} reshape(bf16[256,2,32,32]{3,2,1,0:T(8,128)(2,1)} %bitcast.299) | data formatting | bytes 2097152
  469.6 7.0 reshape.279
  476.6 6.7 copy.104
  492.1 7.0 reshape.277
  499.1 6.7 copy.98
  518.3 74.5 %all-reduce.1 = (f32[]{:T(128)}, f32[]{:T(128)}, f32[]{:T(128)}, f32[]{:T(128)}) all-reduce(f32[]{:T(128)} %get-tuple-element.20, f32[]{:T(128)} %get-tuple-element.16, f32[]{:T(128)} %get-tuple-element.15, f32[]{:T(128)} %get-tuple-element.19), channel_id=1, replica_groups=mesh['coil'=32,'slab'=8] {'coil','slab'}, use_global_device_ids=true, to_apply=%region_6.7 | all-reduce | flops 4 | bytes 32 | tf_op jit(solution)/shard_map/psum | solution.py:119
  597.4 140.0 %psum.55 = f32[2,32,32]{2,1,0:T(8,128)S(1)} all-reduce(f32[2,32,32]{2,1,0:T(8,128)S(1)} %pad_maximum_fusion.7), channel_id=1, replica_groups=mesh['coil'=32,'slab'=8] {'coil'}, use_global_device_ids=true, to_apply=%region_17.18 | all-reduce | flops 2048 | bytes 16384 | tf_op jit(solution)/shard_map/psum | solution.py:128
  (81 shorter events, 110.0 us)
Async XLA Ops:
  7.2 83.4 %all-gather.4.cloned.1.call-start = ((), (), s32[]{:S(2)}) async-start(), calls=%async_computation.4 | async-start | bytes 1081344 | tf_op jit(solution)/shard_map/all_gather | solution.py:74
  9.4 169.6 %all-gather.8.cloned.1.call-start = ((), (), s32[]{:S(2)}) async-start(), calls=%async_computation.6 | async-start | bytes 1081344 | tf_op jit(solution)/shard_map/all_gather | solution.py:74
  16.2 77.7 %copy-start.3 = (bf16[1,256,2,256]{3,1,0,2:T(8,128)(2,1)}, bf16[1,256,2,256]{3,1,0,2:T(8,128)(2,1)S(1)}, u32[]{:S(2)}) copy-start(bf16[1,256,2,256]{3,1,0,2:T(8,128)(2,1)S(1)} %get-tuple-element.47) | copy-start | bytes 786436
  112.1 6.5 copy-start.8
  112.2 6.6 copy-start.7
  112.2 20.0 %all-to-all-start = ((bf16[8,2,32768]{2,1,0:T(2,128)(2,1)}), bf16[8,2,32768]{2,1,0:T(2,128)(2,1)}, u32[]{:S(2)}, u32[]{:S(2)}) async-start(bf16[8,2,32768]{2,1,0:T(2,128)(2,1)} %reshape.272), calls=%async_computation | async-start | bytes 2097152 | tf_op jit(solution)/shard_map/all_to_all | solution.py:80
  152.0 4.4 copy-start.6
  173.2 20.2 %all-to-all-start.1 = ((bf16[8,2,32768]{2,1,0:T(2,128)(2,1)}), bf16[8,2,32768]{2,1,0:T(2,128)(2,1)}, u32[]{:S(2)}, u32[]{:S(2)}) async-start(bf16[8,2,32768]{2,1,0:T(2,128)(2,1)} %reshape.274), calls=%async_computation.1 | async-start | bytes 2097152 | tf_op jit(solution)/shard_map/all_to_all | solution.py:95
  178.7 189.4 %all-reduce.5.cloned.1.call-start = ((), (), s32[]{:S(2)}) async-start(), calls=%async_computation.7 | async-start | bytes 2097152
  213.4 2.2 copy-start.5
  215.6 1.6 copy-start.1
  219.2 1.7 copy-start.9
  219.2 148.9 %copy-start.4 = (f32[1,2,32,256]{3,2,1,0:T(8,128)S(1)}, f32[1,2,32,256]{3,2,1,0:T(8,128)}, u32[]{:S(2)}) copy-start(f32[1,2,32,256]{3,2,1,0:T(8,128)} %param.6) | copy-start | bytes 196612
  220.8 224.0 %all-gather.6.cloned.1.call-start = ((), (), s32[]{:S(2)}) async-start(), calls=%async_computation.5 | async-start | bytes 1081344 | tf_op jit(solution)/shard_map/all_gather | solution.py:74
  389.2 75.6 %all-to-all-start.3 = ((bf16[8,2,32768]{2,1,0:T(2,128)(2,1)}), bf16[8,2,32768]{2,1,0:T(2,128)(2,1)}, u32[]{:S(2)}, u32[]{:S(2)}) async-start(bf16[8,2,32768]{2,1,0:T(2,128)(2,1)} %reshape.278), calls=%async_computation.3 | async-start | bytes 2097152 | tf_op jit(solution)/shard_map/all_to_all | solution.py:80
  464.8 27.3 %all-to-all-start.2 = ((bf16[8,2,32768]{2,1,0:T(2,128)(2,1)}), bf16[8,2,32768]{2,1,0:T(2,128)(2,1)}, u32[]{:S(2)}, u32[]{:S(2)}) async-start(bf16[8,2,32768]{2,1,0:T(2,128)(2,1)} %reshape.276), calls=%async_computation.2 | async-start | bytes 2097152 | tf_op jit(solution)/shard_map/all_to_all | solution.py:80
  483.3 5.4 copy-start.2
  505.8 6.3 copy-start
Sparse Core Ops, SparseCore 0:
  11.1 79.3 all-gather.3
  93.1 73.8 all-gather.7
  221.0 147.1 all-reduce.4
  371.2 73.5 all-gather.5
where the time goes:
time: 763 us; the launch traced here: 753 us
  blocking collectives  288 us (38%)
  waiting for transfers between devices  219 us (29%)
  local copies, waits for them, and re-layouts  143 us (19%)
  other arithmetic  33.3 us (4%)
  matrix products  27.2 us (4%)
  between operations  21.9 us (3%)
  starting transfers between devices  21.2 us (3%)
    psum x1, blocking collectives, shards(): lax.psum(jnp.stack([line_terms(first_k), line_terms(second_k)]), 'coil')  140 us
    all_gather x3, waiting for transfers between devices, gathered_front(): return front(lax.all_gather(shard, 'coil', axis=0, tiled=True))  125 us
    psum x1, blocking collectives, shards(): lax.psum((jnp.sum(residual * residual), jnp.sum(residual * direction), jn...  74.5 us
    psum x1, blocking collectives, shards(): lax.psum((jnp.sum(direction * direction), jnp.sum(first_w * first_w)), both)  73.8 us
    unnamed x5, waiting for transfers between devices  71.1 us
    unnamed x30, local copies, waits for them, and re-layouts  61.8 us
    all_to_all x6, local copies, waits for them, and re-layouts, to_kspace(): lax.all_to_all(mixed, 'slab', split_axis=3, concat_axis=2, tiled=True)  38 us
    convert_element_type x3, local copies, waits for them, and re-layouts, to_kspace(): mixed = jnp.einsum('nixk,inom->moxk', rows, z_fwd, preferred_element_type...  21 us
  transfers between devices with their start and end apart: 8, of which 5 were waited for; matrix products, arithmetic and copies ran while one was open for 18% of the time, Pallas kernels for 0%

commit v1 on v0

--- a/solution.py
+++ b/solution.py
@@ -9,6 +9,11 @@
 NZ = 32
 ITERS = 2
 DAMPING = 0.2
+
+
+def exchange_gather(x, name, along):
+    sent = jnp.stack([x] * lax.axis_size(name))
+    return jnp.concatenate(lax.all_to_all(sent, name, 0, 0), axis=along)
 
 
 def dft_table(length, sign):
@@ -71,7 +76,7 @@
         ).astype(jnp.bfloat16)
 
     def gathered_front(shard):
-        return front(lax.all_gather(shard, "coil", axis=0, tiled=True))
+        return front(exchange_gather(shard, "coil", 0))
 
     def to_kspace(rows):
         mixed = jnp.einsum(

time: 763 us -> 698 us (0.915)
  waiting for transfers between devices: 219 us -> 125 us
  starting transfers between devices: 21.2 us -> 44.6 us
    all_gather x3 -> x0, waiting for transfers between devices: 125 us -> none  [gathered_front(): return front(lax.all_gather(shard, 'coil', axis=0, tiled=True))]
    all_to_all x0 -> x3, waiting for transfers between devices: none -> 28.3 us  [exchange_gather(): return jnp.concatenate(lax.all_to_all(sent, name, 0, 0), axis=along)]
    all_to_all x0 -> x3, starting transfers between devices: none -> 23.6 us  [exchange_gather(): return jnp.concatenate(lax.all_to_all(sent, name, 0, 0), axis=along)]
    unnamed x5 -> x2, waiting for transfers between devices: 71.1 us -> 71.7 us
    unnamed x30 -> x40, local copies, waits for them, and re-layouts: 61.8 us -> 62 us
  transfers between devices with their start and end apart: 8 -> 8, of which waited for: 5 -> 5; matrix products, arithmetic and copies ran while one was open for 18% -> 17% of each run, Pallas kernels for 0% -> 0%
where the time goes in v1:
time: 698 us; the launch traced here: 688 us
  blocking collectives  293 us (42%)
  local copies, waits for them, and re-layouts  146 us (21%)
  waiting for transfers between devices  125 us (18%)
  starting transfers between devices  44.6 us (6%)
  other arithmetic  30.1 us (4%)
  matrix products  27.1 us (4%)
  between operations  22.2 us (3%)
    psum x1, blocking collectives, shards(): lax.psum(jnp.stack([line_terms(first_k), line_terms(second_k)]), 'coil')  142 us
    psum x1, blocking collectives, shards(): lax.psum((jnp.sum(direction * direction), jnp.sum(first_w * first_w)), both)  76.9 us
    psum x1, blocking collectives, shards(): lax.psum((jnp.sum(residual * residual), jnp.sum(residual * direction), jn...  74.4 us
    unnamed x2, waiting for transfers between devices  71.7 us
    unnamed x40, local copies, waits for them, and re-layouts  62 us
    all_to_all x6, local copies, waits for them, and re-layouts, to_kspace(): lax.all_to_all(mixed, 'slab', split_axis=3, concat_axis=2, tiled=True)  37.8 us
    all_to_all x3, waiting for transfers between devices, exchange_gather(): return jnp.concatenate(lax.all_to_all(sent, name, 0, 0), axis=along)  28.3 us
    all_to_all x3, starting transfers between devices, exchange_gather(): return jnp.concatenate(lax.all_to_all(sent, name, 0, 0), axis=along)  23.6 us
  transfers between devices with their start and end apart: 8, of which 5 were waited for; matrix products, arithmetic and copies ran while one was open for 17% of the time, Pallas kernels for 0%

profile of v1, /device:TPU:2, one launch (start us, length us, event | category | flops | bytes accessed | tf_op | source)
XLA Modules:
  0.0 688.3 jit_solution(16948224562066434939)
XLA Ops:
  9.8 11.5 %all-to-all-start = ((bf16[32,1,2,32,256]{4,3,2,1,0:T(8,128)(2,1)}), bf16[32,1,2,32,256]{4,3,2,1,0:T(8,128)(2,1)S(1)}, u32[]{:S(2)}, u32[]{:S(2)}) async-start(bf16[32,1,2,32,256]{4,3,2,1,0:T(8,128)(2,1)} %stack.94), calls=%async_computation | async-start | bytes 2097152 | tf_op jit(solution)/shard_map/all_to_all | solution.py:16
  26.3 23.1 %all-to-all-done = bf16[32,1,2,32,256]{4,3,2,1,0:T(8,128)(2,1)S(1)} async-done(((bf16[32,1,2,32,256]{4,3,2,1,0:T(8,128)(2,1)}), bf16[32,1,2,32,256]{4,3,2,1,0:T(8,128)(2,1)S(1)}, u32[]{:S(2)}, u32[]{:S(2)}) %all-to-all-start) | async-done | bytes 1048608 | tf_op jit(solution)/shard_map/all_to_all | solution.py:16
  54.3 7.2 %copy.46 = bf16[32,2,32,256]{0,2,1,3:T(8,128)(2,1)} copy(bf16[32,2,32,256]{3,0,2,1:T(8,128)(2,1)} %fusion.4) | data formatting | bytes 2097152 | tf_op jit(solution)/shard_map/convert_element_type | solution.py:84
  61.6 7.8 %reshape.293 = bf16[8,2,32768]{2,1,0:T(2,128)(2,1)} reshape(bf16[256,2,32,32]{3,2,1,0:T(8,128)(2,1)} %bitcast.309) | data formatting | bytes 2097152
  74.4 14.5 %all-to-all-done.1 = bf16[8,2,32768]{2,1,0:T(2,128)(2,1)S(1)} async-done(((bf16[8,2,32768]{2,1,0:T(2,128)(2,1)}), bf16[8,2,32768]{2,1,0:T(2,128)(2,1)S(1)}, u32[]{:S(2)}, u32[]{:S(2)}) %all-to-all-start.1) | async-done | bytes 1048608 | tf_op jit(solution)/shard_map/all_to_all | solution.py:85
  100.1 7.0 %reshape.294 = bf16[256,2,32,32]{3,2,1,0:T(8,128)(2,1)} reshape(bf16[8,2,32768]{2,1,0:T(2,128)(2,1)} %copy-done.3) | data formatting | bytes 2097152
  107.1 6.6 copy.47
  126.0 7.2 %copy.50 = bf16[32,2,256,32]{3,0,1,2:T(8,128)(2,1)} copy(bf16[32,2,256,32]{2,3,0,1:T(8,128)(2,1)} %fusion.9) | data formatting | bytes 2097152 | tf_op jit(solution)/shard_map/convert_element_type | solution.py:99
  133.3 7.8 %reshape.295 = bf16[8,2,32768]{2,1,0:T(2,128)(2,1)} reshape(bf16[256,2,32,32]{3,2,1,0:T(8,128)(2,1)} %bitcast.310) | data formatting | bytes 2097152
  150.4 10.9 %all-to-all-done.2 = bf16[8,2,32768]{2,1,0:T(2,128)(2,1)} async-done(((bf16[8,2,32768]{2,1,0:T(2,128)(2,1)}), bf16[8,2,32768]{2,1,0:T(2,128)(2,1)}, u32[]{:S(2)}, u32[]{:S(2)}) %all-to-all-start.2) | async-done | bytes 1048608 | tf_op jit(solution)/shard_map/all_to_all | solution.py:100
  161.3 7.0 %reshape.296 = bf16[256,2,32,32]{3,2,1,0:T(8,128)(2,1)} reshape(bf16[8,2,32768]{2,1,0:T(2,128)(2,1)} %all-to-all-done.2) | data formatting | bytes 2097152
  168.3 6.9 copy.124
  189.5 76.9 %all-reduce.2 = (f32[]{:T(128)}, f32[]{:T(128)}) all-reduce(f32[]{:T(128)} %get-tuple-element.46, f32[]{:T(128)} %get-tuple-element.37), channel_id=1, replica_groups=mesh['coil'=32,'slab'=8] {'coil','slab'}, use_global_device_ids=true, to_apply=%region_1.2 | all-reduce | flops 2 | bytes 16 | tf_op jit(solution)/shard_map/psum | solution.py:93
  268.3 71.7 %all-reduce.5.cloned.1.call-done = bf16[32,2,32,256]{3,2,0,1:T(8,128)(2,1)} async-done(((bf16[32,2,32,256]{3,2,0,1:T(8,128)(2,1)}), bf16[32,2,32,256]{3,2,0,1:T(8,128)(2,1)}) %all-reduce.5.cloned.1.call-update) | async-done | bytes 1048592
  352.6 7.2 %copy.67 = bf16[32,2,32,256]{0,2,1,3:T(8,128)(2,1)} copy(bf16[32,2,32,256]{3,0,2,1:T(8,128)(2,1)} %fusion.7) | data formatting | bytes 2097152 | tf_op jit(solution)/shard_map/convert_element_type | solution.py:84
  359.8 7.8 %reshape.299 = bf16[8,2,32768]{2,1,0:T(2,128)(2,1)} reshape(bf16[256,2,32,32]{3,2,1,0:T(8,128)(2,1)} %bitcast.311) | data formatting | bytes 2097152
  383.3 6.5 copy.61
  389.8 7.8 %reshape.297 = bf16[8,2,32768]{2,1,0:T(2,128)(2,1)} reshape(bf16[256,2,32,32]{3,2,1,0:T(8,128)(2,1)} %bitcast.312) | data formatting | bytes 2097152
  402.7 7.0 %reshape.300 = bf16[256,2,32,32]{3,2,1,0:T(8,128)(2,1)} reshape(bf16[8,2,32768]{2,1,0:T(2,128)(2,1)} %all-to-all-done.6) | data formatting | bytes 2097152
  409.7 6.6 copy.68
  425.1 7.0 %reshape.298 = bf16[256,2,32,32]{3,2,1,0:T(8,128)(2,1)} reshape(bf16[8,2,32768]{2,1,0:T(2,128)(2,1)} %all-to-all-done.4) | data formatting | bytes 2097152
  432.2 6.6 copy.62
  451.3 74.4 %all-reduce.1 = (f32[]{:T(128)}, f32[]{:T(128)}, f32[]{:T(128)}, f32[]{:T(128)}) all-reduce(f32[]{:T(128)} %get-tuple-element.17, f32[]{:T(128)} %get-tuple-element.13, f32[]{:T(128)} %get-tuple-element.12, f32[]{:T(128)} %get-tuple-element.16), channel_id=1, replica_groups=mesh['coil'=32,'slab'=8] {'coil','slab'}, use_global_device_ids=true, to_apply=%region_6.7 | all-reduce | flops 4 | bytes 32 | tf_op jit(solution)/shard_map/psum | solution.py:124
  530.4 141.6 %psum.55 = f32[2,32,32]{2,1,0:T(8,128)S(1)} all-reduce(f32[2,32,32]{2,1,0:T(8,128)S(1)} %pad_maximum_fusion.7), channel_id=1, replica_groups=mesh['coil'=32,'slab'=8] {'coil'}, use_global_device_ids=true, to_apply=%region_17.18 | all-reduce | flops 2048 | bytes 16384 | tf_op jit(solution)/shard_map/psum | solution.py:133
  (91 shorter events, 127.2 us)
Async XLA Ops:
  9.8 39.5 %all-to-all-start = ((bf16[32,1,2,32,256]{4,3,2,1,0:T(8,128)(2,1)}), bf16[32,1,2,32,256]{4,3,2,1,0:T(8,128)(2,1)S(1)}, u32[]{:S(2)}, u32[]{:S(2)}) async-start(bf16[32,1,2,32,256]{4,3,2,1,0:T(8,128)(2,1)} %stack.94), calls=%async_computation | async-start | bytes 2097152 | tf_op jit(solution)/shard_map/all_to_all | solution.py:16
  21.3 4.3 copy-start.5
  21.6 29.7 %copy-start.12 = (bf16[1,32,2,32]{1,3,0,2:T(8,128)(2,1)}, bf16[1,32,2,32]{1,3,0,2:T(8,128)(2,1)S(1)}, u32[]{:S(2)}) copy-start(bf16[1,32,2,32]{1,3,0,2:T(8,128)(2,1)S(1)} %get-tuple-element.55) | copy-start | bytes 12292
  50.0 1.4 copy-start.4
  69.4 5.0 copy-start.10
  69.4 19.4 %all-to-all-start.1 = ((bf16[8,2,32768]{2,1,0:T(2,128)(2,1)}), bf16[8,2,32768]{2,1,0:T(2,128)(2,1)S(1)}, u32[]{:S(2)}, u32[]{:S(2)}) async-start(bf16[8,2,32768]{2,1,0:T(2,128)(2,1)} %reshape.293), calls=%async_computation.1 | async-start | bytes 2097152 | tf_op jit(solution)/shard_map/all_to_all | solution.py:85
  88.9 9.4 %copy-start.3 = (bf16[8,2,32768]{2,1,0:T(2,128)(2,1)}, bf16[8,2,32768]{2,1,0:T(2,128)(2,1)S(1)}, u32[]{:S(2)}) copy-start(bf16[8,2,32768]{2,1,0:T(2,128)(2,1)S(1)} %all-to-all-done.1) | copy-start | bytes 3145732
  90.1 8.2 %copy-start.11 = (s32[32,32]{1,0:T(8,128)S(1)}, s32[32,32]{1,0:T(8,128)}, u32[]{:S(2)}) copy-start(s32[32,32]{1,0:T(8,128)} %param.11) | copy-start | bytes 12292
  90.1 8.3 %copy-start.9 = (f32[32,32]{1,0:T(8,128)S(1)}, f32[32,32]{1,0:T(8,128)}, u32[]{:S(2)}) copy-start(f32[32,32]{1,0:T(8,128)} %param.10) | copy-start | bytes 12292
  90.1 51.0 %all-to-all-start.5 = ((bf16[32,1,2,32,256]{4,3,2,1,0:T(8,128)(2,1)}), bf16[32,1,2,32,256]{4,3,2,1,0:T(8,128)(2,1)}, u32[]{:S(2)}, u32[]{:S(2)}) async-start(bf16[32,1,2,32,256]{4,3,2,1,0:T(8,128)(2,1)} %stack.109), calls=%async_computation.5 | async-start | bytes 2097152 | tf_op jit(solution)/shard_map/all_to_all | solution.py:16
  119.9 4.4 copy-start.8
  141.1 20.2 %all-to-all-start.2 = ((bf16[8,2,32768]{2,1,0:T(2,128)(2,1)}), bf16[8,2,32768]{2,1,0:T(2,128)(2,1)}, u32[]{:S(2)}, u32[]{:S(2)}) async-start(bf16[8,2,32768]{2,1,0:T(2,128)(2,1)} %reshape.295), calls=%async_computation.2 | async-start | bytes 2097152 | tf_op jit(solution)/shard_map/all_to_all | solution.py:100
  146.7 193.3 %all-reduce.5.cloned.1.call-start = ((), (), s32[]{:S(2)}) async-start(), calls=%async_computation.7 | async-start | bytes 2097152
  181.3 2.2 copy-start.7
  183.5 1.6 copy-start.1
  187.2 1.6 copy-start.14
  187.2 152.8 %copy-start.6 = (f32[1,2,32,256]{3,2,1,0:T(8,128)S(1)}, f32[1,2,32,256]{3,2,1,0:T(8,128)}, u32[]{:S(2)}) copy-start(f32[1,2,32,256]{3,2,1,0:T(8,128)} %param.6) | copy-start | bytes 196612
  188.8 160.5 %copy-start.13 = (bf16[1,32,2,32]{1,3,0,2:T(8,128)(2,1)S(1)}, bf16[1,32,2,32]{1,3,0,2:T(8,128)(2,1)}, u32[]{:S(2)}) copy-start(bf16[1,32,2,32]{1,3,0,2:T(8,128)(2,1)} %copy-done.12) | copy-start | bytes 12292
  343.3 29.5 %all-to-all-start.3 = ((bf16[32,1,2,32,256]{4,3,2,1,0:T(8,128)(2,1)}), bf16[32,1,2,32,256]{4,3,2,1,0:T(8,128)(2,1)}, u32[]{:S(2)}, u32[]{:S(2)}) async-start(bf16[32,1,2,32,256]{4,3,2,1,0:T(8,128)(2,1)} %stack.107), calls=%async_computation.3 | async-start | bytes 2097152 | tf_op jit(solution)/shard_map/all_to_all | solution.py:16
  372.8 24.8 %all-to-all-start.6 = ((bf16[8,2,32768]{2,1,0:T(2,128)(2,1)}), bf16[8,2,32768]{2,1,0:T(2,128)(2,1)}, u32[]{:S(2)}, u32[]{:S(2)}) async-start(bf16[8,2,32768]{2,1,0:T(2,128)(2,1)} %reshape.299), calls=%async_computation.6 | async-start | bytes 2097152 | tf_op jit(solution)/shard_map/all_to_all | solution.py:85
  397.6 27.6 %all-to-all-start.4 = ((bf16[8,2,32768]{2,1,0:T(2,128)(2,1)}), bf16[8,2,32768]{2,1,0:T(2,128)(2,1)}, u32[]{:S(2)}, u32[]{:S(2)}) async-start(bf16[8,2,32768]{2,1,0:T(2,128)(2,1)} %reshape.297), calls=%async_computation.4 | async-start | bytes 2097152 | tf_op jit(solution)/shard_map/all_to_all | solution.py:85
  416.3 5.4 copy-start.2
  438.8 6.3 copy-start
Sparse Core Ops, SparseCore 0:
  188.9 151.0 all-reduce.4
